TPU v7x, 128 devices: a whole 4x4x4 slice. The times are simulated.
128 devices in a mesh: freq: 8 (over x, core), blk: 16 (over y, z).
Axes of the slice: x: 4, y: 4, z: 4, core: 2. Of those that a mesh axis runs over, the one named last changes fastest.
Arguments:
- sky_maps: bfloat16 [8, 256, 32, 8192], P('freq', 'blk'), may hold values from -24 to 24
- legendre: bfloat16 [128, 256, 4096], P('blk')
- mode_values: int32 [128], replicated, may hold values from 0 to 4095, as said below
- cycle_order: int32 [256], replicated, may hold values from 0 to 255, each once
- bin_widths: int32 [128], replicated, may hold values from 1 to 512, 4096 in all
Outputs:
- cleaned: float32 [32, 2, 128, 4096], P(None, None, None, ('freq', 'blk'))
Inputs may be any that keep to these rules, and one draw needn't show every extreme that they name: Distinct values, 0 and 4095 among them; legendre[s, q, l] is zero wherever l < mode_values[s]. `cycle_order`: each cycle index once.
All inputs are finite; a program needn't handle non-finite values.
Results may differ from a plain program's by a relative error of at most 0.0036.
Values may be sent and summed in bfloat16 or wider, within the bound.
A program may use at most 192 MiB of HBM per device.

v0:
```python
import math
import jax
import jax.numpy as jnp
from jax import lax
from jax.sharding import PartitionSpec as P


def build_trig(mode_values, pixel_count):
    pixels = jnp.arange(pixel_count, dtype=jnp.int32)
    phase_index = pixels[:, None] * mode_values[None, :] % pixel_count
    angles = phase_index.astype(jnp.float32) * jnp.float32(2.0 * math.pi / pixel_count)
    factor = jnp.float32(pixel_count ** (-0.5))
    return (jnp.cos(angles) * factor, -jnp.sin(angles) * factor)


def ilc_weights(spectra):
    chan_count = spectra.shape[1]
    trace_value = jnp.trace(spectra, axis1=1, axis2=2)
    identity = jnp.eye(chan_count, dtype=jnp.float32)
    loaded = (
        spectra
        + (jnp.float32(0.1) * trace_value / jnp.float32(chan_count))[:, None, None] * identity[None]
    )
    lower_factor = jnp.linalg.cholesky(loaded)
    unit_vector = jnp.ones(spectra.shape[:2] + (1,), jnp.float32)
    forward = jax.scipy.linalg.solve_triangular(lower_factor, unit_vector, lower=True)
    solved = jax.scipy.linalg.solve_triangular(lower_factor, forward, trans=1, lower=True)[..., 0]
    return solved / jnp.sum(solved, axis=1, keepdims=True)


def project_mode(left_side, table_rows):
    dims = (((0,), (0,)), ((), ()))
    return lax.dot_general(left_side, table_rows, dims, preferred_element_type=jnp.float32).astype(
        jnp.bfloat16
    )


def clean_band(pieces, ell_start, multiplier, bin_widths):
    chan_count = pieces.shape[0]
    ell_span = pieces.shape[4]
    weighted = pieces * multiplier.astype(jnp.bfloat16)[None, None, None, :, None]
    per_ell = jnp.einsum("ikcsl,jkcsl->ijl", weighted, pieces, preferred_element_type=jnp.float32)
    bin_ends = jnp.cumsum(bin_widths)
    begins = bin_ends - bin_widths
    ell_values = ell_start + jnp.arange(ell_span, dtype=jnp.int32)
    onehot = (
        (ell_values[:, None] >= begins[None, :]) & (ell_values[:, None] < bin_ends[None, :])
    ).astype(jnp.float32)
    partial_value = jnp.dot(
        per_ell.reshape(chan_count * chan_count, ell_span), onehot, precision=lax.Precision.HIGHEST
    )
    spectra = lax.psum(partial_value, ("freq", "blk"))
    weights = ilc_weights(spectra.T.reshape(bin_widths.shape[0], chan_count, chan_count))
    per_ell_weights = jnp.dot(onehot, weights, precision=lax.Precision.HIGHEST)
    return jnp.einsum(
        "ikcsl,li->kcsl",
        pieces.astype(jnp.float32),
        per_ell_weights,
        precision=lax.Precision.HIGHEST,
    )


def on_device(sky_maps, legendre, mode_values, cycle_order, bin_widths):
    groups = lax.axis_size("blk")
    per_device = legendre.shape[0]
    row_count = sky_maps.shape[1]
    map_count = sky_maps.shape[2]
    pixel_count = sky_maps.shape[3]
    ell_count = legendre.shape[2]
    cos_part, sin_part = build_trig(mode_values, pixel_count)
    fourier = jnp.stack(
        [
            cos_part.reshape(pixel_count, groups, per_device),
            sin_part.reshape(pixel_count, groups, per_device),
        ],
        axis=2,
    )
    fourier = fourier.reshape(pixel_count, groups * 2 * per_device).astype(jnp.bfloat16)
    fourier_rows = jnp.dot(
        sky_maps.reshape(row_count * map_count, pixel_count),
        fourier,
        preferred_element_type=jnp.float32,
    )
    fourier_rows = fourier_rows.astype(jnp.bfloat16).reshape(
        row_count, map_count, groups * 2 * per_device
    )
    inverse = jnp.argsort(cycle_order)
    block_index = lax.axis_index("blk")
    freq_index = lax.axis_index("freq")
    multiplier = jnp.where(mode_values > 0, 2.0, 1.0).astype(jnp.float32)
    gathered = lax.all_to_all(fourier_rows, "blk", split_axis=2, concat_axis=0, tiled=True)
    ordered = gathered[inverse]
    item_count = ordered.shape[1]
    results = []
    for slot_index in range(per_device):
        left_side = ordered[:, :, slot_index::per_device].reshape(ordered.shape[0], item_count * 2)
        results.append(project_mode(left_side, legendre[slot_index]))
    stacked = jnp.stack(results, axis=1)
    coeffs = stacked.reshape(item_count, 2, per_device, ell_count)
    pieces = lax.all_to_all(
        lax.all_to_all(coeffs[None], "freq", split_axis=4, concat_axis=0, tiled=True),
        "blk",
        split_axis=4,
        concat_axis=3,
        tiled=True,
    )
    ell_start = (freq_index * groups + block_index) * pieces.shape[4]
    cleaned = clean_band(pieces, ell_start, multiplier, bin_widths)
    return cleaned


def solution(mesh):
    return jax.shard_map(
        on_device,
        mesh=mesh,
        in_specs=(P("freq", "blk", None, None), P("blk", None, None), P(), P(), P()),
        out_specs=P(None, None, None, ("freq", "blk")),
        check_vma=False,
    )
```

profile of v0, /device:TPU:1, one launch (start us, length us, event | category | flops | bytes accessed | tf_op | source)
XLA Modules:
  0.0 697.8 jit_solution(2399682190589871519)
XLA Ops:
  0.7 18.3 %multiply_convert_fusion.1 = (bf16[8192,16,1,8]{0,3,2,1:T(8,128)(2,1)S(1)}, bf16[8192,16,1,8]{0,3,2,1:T(8,128)(2,1)S(1)}) fusion(s32[16,8]{1,0:T(8,128)S(1)} %mul.96), kind=kLoop, calls=%fused_computation.19 | loop fusion | flops 19922944 | bytes 4194816 | tf_op jit(solution)/shard_map/convert
  19.5 3.0 copy-done.3
  22.4 2.4 fusion.22
  25.9 1.7 reshape.236
  27.6 8.6 %all-to-all-start = ((bf16[16,2,4096]{2,1,0:T(2,128)(2,1)}), bf16[16,2,4096]{2,1,0:T(2,128)(2,1)S(1)}, u32[]{:S(2)}, u32[]{:S(2)}) async-start(bf16[16,2,4096]{2,1,0:T(2,128)(2,1)} %reshape.236), calls=%async_computation | async-start | bytes 524288 | tf_op jit(solution)/shard_map/all_to_all | solution.py:91
  36.2 3.2 sort.17
  39.4 4.2 all-to-all-done
  45.3 1.4 slice.66
  46.7 1.4 slice.68
  48.2 1.4 slice.70
  49.6 1.4 slice.72
  51.0 1.4 slice.74
  52.5 1.4 slice.76
  53.9 1.4 slice.78
  56.9 2.1 convolution_convert_fusion.7
  59.3 7.4 %copy.174 = bf16[1,32,2,1,4096]{1,3,2,0,4:T(2,128)(2,1)} copy(bf16[1,32,2,1,4096]{4,2,1,3,0:T(2,128)(2,1)S(1)} %stack.32) | data formatting | bytes 1048576 | tf_op jit(solution)/shard_map/stack | solution.py:98
  66.9 2.1 convolution_convert_fusion.6
  69.3 7.4 %copy.175 = bf16[1,32,2,1,4096]{1,3,2,0,4:T(2,128)(2,1)} copy(bf16[1,32,2,1,4096]{4,2,1,3,0:T(2,128)(2,1)S(1)} %stack.33) | data formatting | bytes 1048576 | tf_op jit(solution)/shard_map/stack | solution.py:98
  76.8 2.1 convolution_convert_fusion.5
  79.2 7.4 %copy.176 = bf16[1,32,2,1,4096]{1,3,2,0,4:T(2,128)(2,1)} copy(bf16[1,32,2,1,4096]{4,2,1,3,0:T(2,128)(2,1)S(1)} %stack.34) | data formatting | bytes 1048576 | tf_op jit(solution)/shard_map/stack | solution.py:98
  86.8 2.1 convolution_convert_fusion.4
  89.2 7.4 %copy.177 = bf16[1,32,2,1,4096]{1,3,2,0,4:T(2,128)(2,1)} copy(bf16[1,32,2,1,4096]{4,2,1,3,0:T(2,128)(2,1)S(1)} %stack.35) | data formatting | bytes 1048576 | tf_op jit(solution)/shard_map/stack | solution.py:98
  96.7 2.1 convolution_convert_fusion.3
  99.1 7.4 %copy.178 = bf16[1,32,2,1,4096]{1,3,2,0,4:T(2,128)(2,1)} copy(bf16[1,32,2,1,4096]{4,2,1,3,0:T(2,128)(2,1)S(1)} %stack.36) | data formatting | bytes 1048576 | tf_op jit(solution)/shard_map/stack | solution.py:98
  106.6 2.1 convolution_convert_fusion.2
  109.1 7.4 %copy.179 = bf16[1,32,2,1,4096]{1,3,2,0,4:T(2,128)(2,1)} copy(bf16[1,32,2,1,4096]{4,2,1,3,0:T(2,128)(2,1)S(1)} %stack.37) | data formatting | bytes 1048576 | tf_op jit(solution)/shard_map/stack | solution.py:98
  116.6 2.1 convolution_convert_fusion.1
  119.0 7.4 %copy.180 = bf16[1,32,2,1,4096]{1,3,2,0,4:T(2,128)(2,1)} copy(bf16[1,32,2,1,4096]{4,2,1,3,0:T(2,128)(2,1)S(1)} %stack.38) | data formatting | bytes 1048576 | tf_op jit(solution)/shard_map/stack | solution.py:98
  126.5 2.1 convolution_convert_fusion
  128.9 7.4 %copy.181 = bf16[1,32,2,1,4096]{1,3,2,0,4:T(2,128)(2,1)} copy(bf16[1,32,2,1,4096]{4,2,1,3,0:T(2,128)(2,1)S(1)} %stack.39) | data formatting | bytes 1048576 | tf_op jit(solution)/shard_map/stack | solution.py:98
  136.3 85.4 %stack.40 = bf16[1,32,2,8,4096]{1,3,2,0,4:T(8,128)(2,1)} concatenate(bf16[1,32,2,1,4096]{1,3,2,0,4:T(2,128)(2,1)} %copy.174, bf16[1,32,2,1,4096]{1,3,2,0,4:T(2,128)(2,1)} %copy.175, bf16[1,32,2,1,4096]{1,3,2,0,4:T(2,128)(2,1)} %copy.176, bf16[1,32,2,1,4096]{1,3,2,0,4:T(2,128)(2,1)} %copy.177, bf16[1,32,2,1,4096]{1,3,2,0,4:T(2,128)(2,1)} %copy.178, ...), dimensions={3} | concatenate | bytes 8388608 | tf_op jit(solution)/shard_map/stack | solution.py:98
  221.7 18.9 %reshape.238 = bf16[8,2,131072]{2,1,0:T(2,128)(2,1)} reshape(bf16[4096,1,2,8,32]{4,3,2,1,0:T(8,128)(2,1)} %bitcast.108) | data formatting | bytes 8388608
  240.6 55.1 %all_to_all.54 = bf16[8,2,131072]{2,1,0:T(2,128)(2,1)} all-to-all(bf16[8,2,131072]{2,1,0:T(2,128)(2,1)} %reshape.238), channel_id=1, replica_groups=mesh['freq'=8,'blk'=16] {'freq'}, dimensions={0} | all-to-all | bytes 8388608 | tf_op jit(solution)/shard_map/all_to_all | solution.py:101
  295.7 12.4 %reshape.239 = bf16[4096,1,2,8,32]{4,3,2,1,0:T(8,128)(2,1)} reshape(bf16[8,2,131072]{2,1,0:T(2,128)(2,1)} %all_to_all.54) | data formatting | bytes 8388608
  308.2 15.3 %copy.218 = bf16[8,32,2,8,512]{1,3,2,0,4:T(8,128)(2,1)} copy(bf16[8,32,2,8,512]{1,3,2,4,0:T(8,128)(2,1)} %bitcast.109) | data formatting | bytes 8388608 | tf_op jit(solution)/shard_map/all_to_all | solution.py:101
  323.5 20.8 %reshape.240 = bf16[16,2,65536]{2,1,0:T(2,128)(2,1)} reshape(bf16[512,8,2,8,32]{4,3,2,1,0:T(8,128)(2,1)} %bitcast.110) | data formatting | bytes 8388608
  344.2 4.7 all-to-all-start.2
  349.5 59.1 %all-to-all-done.2 = bf16[16,2,65536]{2,1,0:T(2,128)(2,1)} async-done(((bf16[16,2,65536]{2,1,0:T(2,128)(2,1)}), bf16[16,2,65536]{2,1,0:T(2,128)(2,1)}, u32[]{:S(2)}, u32[]{:S(2)}) %all-to-all-start.2) | async-done | bytes 4194336 | tf_op jit(solution)/shard_map/all_to_all | solution.py:100
  408.6 16.0 %reshape.241 = bf16[512,8,2,8,32]{4,3,2,1,0:T(8,128)(2,1)} reshape(bf16[16,2,65536]{2,1,0:T(2,128)(2,1)} %all-to-all-done.2) | data formatting | bytes 8388608
  424.6 36.1 %copy.185 = bf16[8,32,2,16,8,32]{5,4,3,2,1,0:T(8,128)(2,1)} copy(bf16[8,32,2,16,8,32]{1,4,2,0,5,3:T(8,128)(2,1)} %bitcast.111) | data formatting | bytes 8388608 | tf_op jit(solution)/shard_map/all_to_all | solution.py:100
  460.7 14.3 %broadcast_multiply_fusion = bf16[8,32,2,128,32]{4,3,2,1,0:T(8,128)(2,1)} fusion(bf16[128]{0:T(256)(128)(2,1)S(1)} %fusion.35, bf16[8,32,2,16,8,32]{5,4,3,2,1,0:T(8,128)(2,1)} %copy.185), kind=kLoop, calls=%fused_computation.2 | loop fusion | flops 2097152 | bytes 8388864 | tf_op jit(solution)/shard_map/mul | solution.py:41
  475.0 16.1 %copy.187 = bf16[8,32,2,128,32]{3,0,1,2,4:T(8,128)(2,1)} copy(bf16[8,32,2,128,32]{4,3,2,1,0:T(8,128)(2,1)} %broadcast_multiply_fusion) | data formatting | bytes 8388608 | tf_op jit(solution)/shard_map/mul | solution.py:41
  491.1 16.0 %copy.186 = bf16[8,32,2,128,32]{3,0,1,2,4:T(8,128)(2,1)} copy(bf16[8,32,2,128,32]{4,3,2,1,0:T(8,128)(2,1)} %bitcast.107) | data formatting | bytes 8388608 | tf_op jit(solution)/shard_map/all_to_all | solution.py:100
  507.1 6.3 convolution_bitcast_fusion
  513.7 70.2 %psum.7 = f32[128,64]{0,1:T(8,128)S(1)} all-reduce(f32[128,64]{0,1:T(8,128)S(1)} %fusion.23), channel_id=1, replica_groups=mesh['freq'=8,'blk'=16] {'freq','blk'}, use_global_device_ids=true, to_apply=%region_2.3 | all-reduce | flops 8192 | bytes 65536 | tf_op jit(solution)/shard_map/psum | solution.py:52
  584.4 93.9 %custom-call.11 = f32[128,8,8]{2,1,0:T(8,128)S(1)} custom-call(f32[128,8,8]{2,1,0:T(8,128)S(1)} %broadcast_multiply_fusion.1), custom_call_target="Cholesky" | custom-call | tf_op jit(solution)/shard_map/jit(cholesky)/cholesky | solution.py:24
  681.0 13.2 %multiply_reduce_fusion = f32[32,32,2,128]{0,3,2,1:T(8,128)} fusion(f32[32,8]{0,1:T(8,128)S(1)} %fusion.25, bf16[8,32,2,16,8,32]{5,4,3,2,1,0:T(8,128)(2,1)} %copy.185), kind=kLoop, calls=%fused_computation.1 | loop fusion | flops 6029312 | bytes 5243904
  694.2 3.6 copy.207
  (72 shorter events, 12.8 us)
Async XLA Ops:
  19.1 3.4 copy-start.3
  22.4 13.8 %copy-start = (s32[256]{0:T(256)S(1)}, s32[256]{0:T(256)}, u32[]{:S(2)}) copy-start(s32[256]{0:T(256)} %param.8) | copy-start | bytes 3076
  27.6 16.1 %all-to-all-start = ((bf16[16,2,4096]{2,1,0:T(2,128)(2,1)}), bf16[16,2,4096]{2,1,0:T(2,128)(2,1)S(1)}, u32[]{:S(2)}, u32[]{:S(2)}) async-start(bf16[16,2,4096]{2,1,0:T(2,128)(2,1)} %reshape.236), calls=%async_computation | async-start | bytes 524288 | tf_op jit(solution)/shard_map/all_to_all | solution.py:91
  344.2 4.7 copy-start.1
  344.2 5.2 copy-start.2
  344.2 64.3 %all-to-all-start.2 = ((bf16[16,2,65536]{2,1,0:T(2,128)(2,1)}), bf16[16,2,65536]{2,1,0:T(2,128)(2,1)}, u32[]{:S(2)}, u32[]{:S(2)}) async-start(bf16[16,2,65536]{2,1,0:T(2,128)(2,1)} %reshape.240), calls=%async_computation.2 | async-start | bytes 8388608 | tf_op jit(solution)/shard_map/all_to_all | solution.py:100
where the time goes:
time: 711 us; the launch traced here: 698 us
  local copies, waits for them, and re-layouts  324 us (46%)
  other arithmetic  145 us (20%)
  blocking collectives  125 us (18%)
  waiting for transfers between devices  63.3 us (9%)
  matrix products  26.6 us (4%)
  starting transfers between devices  13.3 us (2%)
    another operation x17, local copies, waits for them, and re-layouts, on_device(): stacked = jnp.stack(results, axis=1)  147 us
    another operation x4, other arithmetic, ilc_weights(): lower_factor = jnp.linalg.cholesky(loaded)  94.1 us
    unnamed x15, local copies, waits for them, and re-layouts  73.4 us
    psum x1, blocking collectives, clean_band(): spectra = lax.psum(partial_value, ('freq', 'blk'))  70.2 us
    all_to_all x1, waiting for transfers between devices, on_device(): lax.all_to_all(lax.all_to_all(coeffs[None], 'freq', split_axis=4, concat_...  59.1 us
    all_to_all x1, blocking collectives, on_device(): lax.all_to_all(coeffs[None], 'freq', split_axis=4, concat_axis=0, tiled=T...  55.1 us
    all_to_all x2, local copies, waits for them, and re-layouts, on_device(): lax.all_to_all(lax.all_to_all(coeffs[None], 'freq', split_axis=4, concat_...  52.1 us
    another operation x3, other arithmetic  18.6 us
  transfers between devices with their start and end apart: 2, of which 2 were waited for; matrix products, arithmetic and copies ran while one was open for 1% of the time, Pallas kernels for 0%

commit v1 on v0

--- a/solution.py
+++ b/solution.py
@@ -61,6 +61,16 @@
 
 
 def on_device(sky_maps, legendre, mode_values, cycle_order, bin_widths):
+
+    def replace_flows(row_axis, unit):
+        z1 = jnp.concatenate(
+            lax.all_to_all(
+                jnp.stack(jnp.split(unit, lax.axis_size(row_axis), 4), 0), row_axis, 0, 0
+            ),
+            axis=0,
+        )
+        return z1
+
     groups = lax.axis_size("blk")
     per_device = legendre.shape[0]
     row_count = sky_maps.shape[1]
@@ -98,11 +108,7 @@
     stacked = jnp.stack(results, axis=1)
     coeffs = stacked.reshape(item_count, 2, per_device, ell_count)
     pieces = lax.all_to_all(
-        lax.all_to_all(coeffs[None], "freq", split_axis=4, concat_axis=0, tiled=True),
-        "blk",
-        split_axis=4,
-        concat_axis=3,
-        tiled=True,
+        replace_flows("freq", coeffs[None]), "blk", split_axis=4, concat_axis=3, tiled=True
     )
     ell_start = (freq_index * groups + block_index) * pieces.shape[4]
     cleaned = clean_band(pieces, ell_start, multiplier, bin_widths)

time: 711 us -> 608 us (0.86)
  local copies, waits for them, and re-layouts: 324 us -> 223 us
    another operation x17 -> x9, local copies, waits for them, and re-layouts: 147 us -> 44 us  [on_device(): stacked = jnp.stack(results, axis=1)]
    reshape x0 -> x1, local copies, waits for them, and re-layouts: none -> 28.4 us  [replace_flows(): jnp.concatenate(lax.all_to_all(jnp.stack(jnp.split(unit, lax.axis_size(ro...]
    unnamed x15 -> x20, local copies, waits for them, and re-layouts: 73.4 us -> 49.6 us
    all_to_all x3 -> x2, local copies, waits for them, and re-layouts: 67.4 us -> 52.1 us  [on_device(): lax.all_to_all(replace_flows('freq', coeffs[None]), 'blk', split_axis=4,...]
    slice x16, local copies, waits for them, and re-layouts: 12.2 us -> 20.1 us  [on_device(): ordered[:, :, slot_index::per_device]]
where the time goes in v1:
time: 608 us; the launch traced here: 602 us
  local copies, waits for them, and re-layouts  223 us (37%)
  other arithmetic  145 us (24%)
  blocking collectives  122 us (20%)
  waiting for transfers between devices  66.9 us (11%)
  matrix products  31.4 us (5%)
  starting transfers between devices  13.5 us (2%)
    another operation x4, other arithmetic, ilc_weights(): lower_factor = jnp.linalg.cholesky(loaded)  94.1 us
    psum x1, blocking collectives, clean_band(): spectra = lax.psum(partial_value, ('freq', 'blk'))  67.2 us
    all_to_all x1, waiting for transfers between devices, on_device(): lax.all_to_all(replace_flows('freq', coeffs[None]), 'blk', split_axis=4,...  62.7 us
    all_to_all x1, blocking collectives, replace_flows(): lax.all_to_all(jnp.stack(jnp.split(unit, lax.axis_size(row_axis), 4), 0),...  54.8 us
    all_to_all x2, local copies, waits for them, and re-layouts, on_device(): lax.all_to_all(replace_flows('freq', coeffs[None]), 'blk', split_axis=4,...  52.1 us
    unnamed x20, local copies, waits for them, and re-layouts  49.6 us
    another operation x9, local copies, waits for them, and re-layouts, on_device(): stacked = jnp.stack(results, axis=1)  44 us
    reshape x1, local copies, waits for them, and re-layouts, replace_flows(): jnp.concatenate(lax.all_to_all(jnp.stack(jnp.split(unit, lax.axis_size(ro...  28.4 us
  transfers between devices with their start and end apart: 2, of which 2 were waited for; matrix products, arithmetic and copies ran while one was open for 1% of the time, Pallas kernels for 0%

profile of v1, /device:TPU:1, one launch (start us, length us, event | category | flops | bytes accessed | tf_op | source)
XLA Modules:
  0.0 601.6 jit_solution(7428835626858671512)
XLA Ops:
  0.7 18.3 %multiply_convert_fusion.1 = (bf16[8192,16,1,8]{0,3,2,1:T(8,128)(2,1)S(1)}, bf16[8192,16,1,8]{0,3,2,1:T(8,128)(2,1)S(1)}) fusion(s32[16,8]{1,0:T(8,128)S(1)} %mul.96), kind=kLoop, calls=%fused_computation.19 | loop fusion | flops 19922944 | bytes 4194816 | tf_op jit(solution)/shard_map/convert
  19.5 3.0 copy-done.3
  22.4 2.4 fusion.22
  25.9 1.7 reshape.240
  27.6 8.6 %all-to-all-start = ((bf16[16,2,4096]{2,1,0:T(2,128)(2,1)}), bf16[16,2,4096]{2,1,0:T(2,128)(2,1)S(1)}, u32[]{:S(2)}, u32[]{:S(2)}) async-start(bf16[16,2,4096]{2,1,0:T(2,128)(2,1)} %reshape.240), calls=%async_computation | async-start | bytes 524288 | tf_op jit(solution)/shard_map/all_to_all | solution.py:101
  36.2 3.2 sort.17
  39.4 4.2 all-to-all-done
  45.3 1.4 slice.66
  46.7 1.4 slice.68
  48.2 1.4 slice.70
  49.6 3.6 slice.72
  53.2 3.5 slice.74
  56.7 1.4 slice.76
  58.1 1.4 slice.78
  59.6 1.4 slice.80
  61.1 2.1 convolution_convert_fusion.7
  64.3 2.1 convolution_convert_fusion.6
  67.4 2.9 convolution_convert_fusion.5
  70.3 2.5 stack.79
  72.8 1.7 copy.171
  75.8 2.9 convolution_convert_fusion.4
  78.7 3.7 stack.80
  82.3 1.6 copy.172
  84.0 1.4 reshape.216
  85.3 2.9 convolution_convert_fusion.3
  88.2 3.7 stack.81
  93.3 2.9 convolution_convert_fusion.2
  96.2 3.7 stack.82
  100.0 2.9 convolution_convert_fusion.1
  102.9 3.7 stack.83
  106.7 2.9 convolution_convert_fusion
  109.5 3.7 stack.84
  113.2 21.4 %stack.67 = bf16[1,32,2,8,4096]{4,3,2,1,0:T(8,128)(2,1)} concatenate(bf16[1,32,2,1,4096]{4,3,2,1,0:T(2,128)(2,1)S(1)} %stack.77, bf16[1,32,2,1,4096]{4,3,2,1,0:T(2,128)(2,1)S(1)} %stack.78, bf16[1,32,2,1,4096]{4,3,2,1,0:T(2,128)(2,1)S(1)} %stack.79, bf16[1,32,2,1,4096]{4,3,2,1,0:T(2,128)(2,1)} %stack.80, bf16[1,32,2,1,4096]{4,3,2,1,0:T(2,128)(2,1)} %stack.81, ...), dimensions={3} | concatenate | bytes 8388608 | tf_op jit(solution)/shard_map/stack | solution.py:108
  143.3 54.8 %all_to_all.41 = bf16[8,1,32,2,8,512]{5,4,3,2,1,0:T(8,128)(2,1)} all-to-all(bf16[8,1,32,2,8,512]{5,4,3,2,1,0:T(8,128)(2,1)S(1)} %fusion.23), channel_id=1, replica_groups=mesh['freq'=8,'blk'=16] {'freq'}, dimensions={0} | all-to-all | bytes 8388608 | tf_op jit(solution)/shard_map/all_to_all | solution.py:67
  198.1 28.4 %copy.184 = bf16[8,32,2,8,512]{1,3,2,0,4:T(8,128)(2,1)} copy(bf16[8,32,2,8,512]{4,3,2,1,0:T(8,128)(2,1)} %bitcast.134) | data formatting | bytes 8388608 | tf_op jit(solution)/shard_map/reshape | solution.py:66
  226.5 20.7 %reshape.242 = bf16[16,2,65536]{2,1,0:T(2,128)(2,1)} reshape(bf16[512,8,2,8,32]{4,3,2,1,0:T(8,128)(2,1)} %bitcast.132) | data formatting | bytes 8388608
  247.3 4.9 all-to-all-start.2
  252.8 62.7 %all-to-all-done.2 = bf16[16,2,65536]{2,1,0:T(2,128)(2,1)} async-done(((bf16[16,2,65536]{2,1,0:T(2,128)(2,1)}), bf16[16,2,65536]{2,1,0:T(2,128)(2,1)}, u32[]{:S(2)}, u32[]{:S(2)}) %all-to-all-start.2) | async-done | bytes 4194336 | tf_op jit(solution)/shard_map/all_to_all | solution.py:110
  315.4 16.0 %reshape.243 = bf16[512,8,2,8,32]{4,3,2,1,0:T(8,128)(2,1)} reshape(bf16[16,2,65536]{2,1,0:T(2,128)(2,1)} %all-to-all-done.2) | data formatting | bytes 8388608
  331.5 36.1 %copy.186 = bf16[8,32,2,16,8,32]{5,4,3,2,1,0:T(8,128)(2,1)} copy(bf16[8,32,2,16,8,32]{1,4,2,0,5,3:T(8,128)(2,1)} %bitcast.133) | data formatting | bytes 8388608 | tf_op jit(solution)/shard_map/all_to_all | solution.py:110
  367.6 14.3 %broadcast_multiply_fusion = bf16[8,32,2,128,32]{4,3,2,1,0:T(8,128)(2,1)} fusion(bf16[128]{0:T(256)(128)(2,1)S(1)} %fusion.43, bf16[8,32,2,16,8,32]{5,4,3,2,1,0:T(8,128)(2,1)} %copy.186), kind=kLoop, calls=%fused_computation.2 | loop fusion | flops 2097152 | bytes 8388864 | tf_op jit(solution)/shard_map/mul | solution.py:41
  381.9 16.1 %copy.188 = bf16[8,32,2,128,32]{3,0,1,2,4:T(8,128)(2,1)} copy(bf16[8,32,2,128,32]{4,3,2,1,0:T(8,128)(2,1)} %broadcast_multiply_fusion) | data formatting | bytes 8388608 | tf_op jit(solution)/shard_map/mul | solution.py:41
  397.9 16.0 %copy.187 = bf16[8,32,2,128,32]{3,0,1,2,4:T(8,128)(2,1)} copy(bf16[8,32,2,128,32]{4,3,2,1,0:T(8,128)(2,1)} %bitcast.131) | data formatting | bytes 8388608 | tf_op jit(solution)/shard_map/all_to_all | solution.py:110
  413.9 6.3 %convolution_bitcast_fusion = f32[8,8,32]{0,1,2:T(8,128)S(1)} fusion(bf16[8,32,2,128,32]{3,0,1,2,4:T(8,128)(2,1)} %copy.187, bf16[8,32,2,128,32]{3,0,1,2,4:T(8,128)(2,1)} %copy.188), kind=kOutput, calls=%fused_computation.41 | convolution fusion | flops 33554432 | bytes 8396800 | tf_op jit(solution)/shard_map/ikcsl,jkcsl->ijl/dot_general | solution.py:42
  420.5 67.2 %psum.7 = f32[128,64]{0,1:T(8,128)S(1)} all-reduce(f32[128,64]{0,1:T(8,128)S(1)} %fusion.31), channel_id=1, replica_groups=mesh['freq'=8,'blk'=16] {'freq','blk'}, use_global_device_ids=true, to_apply=%region_2.3 | all-reduce | flops 8192 | bytes 65536 | tf_op jit(solution)/shard_map/psum | solution.py:52
  488.2 93.9 %custom-call.11 = f32[128,8,8]{2,1,0:T(8,128)S(1)} custom-call(f32[128,8,8]{2,1,0:T(8,128)S(1)} %broadcast_multiply_fusion.1), custom_call_target="Cholesky" | custom-call | tf_op jit(solution)/shard_map/jit(cholesky)/cholesky | solution.py:24
  584.9 13.2 %multiply_reduce_fusion = f32[32,32,2,128]{0,3,2,1:T(8,128)} fusion(f32[32,8]{0,1:T(8,128)S(1)} %fusion.33, bf16[8,32,2,16,8,32]{5,4,3,2,1,0:T(8,128)(2,1)} %copy.186), kind=kLoop, calls=%fused_computation.1 | loop fusion | flops 6029312 | bytes 5243904
  598.0 3.6 copy.208
  (70 shorter events, 21.6 us)
Async XLA Ops:
  19.1 3.4 copy-start.3
  22.4 13.8 %copy-start = (s32[256]{0:T(256)S(1)}, s32[256]{0:T(256)}, u32[]{:S(2)}) copy-start(s32[256]{0:T(256)} %param.8) | copy-start | bytes 3076
  27.6 16.1 %all-to-all-start = ((bf16[16,2,4096]{2,1,0:T(2,128)(2,1)}), bf16[16,2,4096]{2,1,0:T(2,128)(2,1)S(1)}, u32[]{:S(2)}, u32[]{:S(2)}) async-start(bf16[16,2,4096]{2,1,0:T(2,128)(2,1)} %reshape.240), calls=%async_computation | async-start | bytes 524288 | tf_op jit(solution)/shard_map/all_to_all | solution.py:101
  247.3 4.9 copy-start.1
  247.3 5.4 copy-start.2
  247.3 68.1 %all-to-all-start.2 = ((bf16[16,2,65536]{2,1,0:T(2,128)(2,1)}), bf16[16,2,65536]{2,1,0:T(2,128)(2,1)}, u32[]{:S(2)}, u32[]{:S(2)}) async-start(bf16[16,2,65536]{2,1,0:T(2,128)(2,1)} %reshape.242), calls=%async_computation.2 | async-start | bytes 8388608 | tf_op jit(solution)/shard_map/all_to_all | solution.py:110
